TPU v7x, 32 devices: a whole 2x2x4 slice. The times are simulated.
32 devices in a mesh: ctx: 8 (over z, y), grp: 4 (over x, core).
Axes of the slice: x: 2, y: 2, z: 4, core: 2. Of those that a mesh axis runs over, the one named last changes fastest.
Arguments:
- streams: bfloat16 [3, 3072, 4096], P(None, 'ctx', 'grp'), may hold values from -400 to 400
- filters: bfloat16 [3, 256, 128], P(None, 'grp'), may hold values from -0.5 to 0.5
- gain: float32 [4096], P('grp'), may hold values from 0.5 to 1.5
Outputs:
- normed: bfloat16 [3072, 4096], P('ctx', 'grp')
All inputs are finite; a program needn't handle non-finite values.
Results may differ from a plain program's by a relative error of at most 0.012.
The roundings to bfloat16 on the way count: a program that leaves them out, or rounds other values in their place, can miss the bound.
Values may be sent and summed in bfloat16 or wider, within the bound.
A program may use at most 128 MiB of HBM per device.

v0:
```python
import functools
import math

import jax
import jax.numpy as jnp
import numpy as np
from jax import lax
from jax.experimental import pallas as pl
from jax.experimental.pallas import tpu as pltpu
from jax.sharding import PartitionSpec as P

HD = 128
LANES = 128
MESH = pl.DeviceIdType.MESH


def fused_kernel(
    n,
    n_grp,
    streams,
    filters,
    gain,
    out,
    buf,
    taps,
    toep,
    feat,
    top,
    total,
    accum,
    sending,
    att,
    sums,
    local_sem,
    send_sem,
    recv_sem,
    back_send,
    back_recv,
    sum_send,
    sum_recv,
):
    me = lax.axis_index("ctx")
    my_grp = lax.axis_index("grp")
    rows = streams.shape[1]
    chans = streams.shape[2]
    groups = filters.shape[1]
    flen = filters.shape[2]
    cols = chans // n
    width = chans // groups
    own_groups = groups // n
    per_tile = LANES // width
    heads = cols // HD

    def col_of(j):
        return pl.ds(pl.multiple_of(j * cols, cols), cols)

    def row_of(i):
        return pl.ds(pl.multiple_of(flen + i * rows, flen), rows)

    barrier = pltpu.get_barrier_semaphore()
    for k in range(1, n):
        pl.semaphore_signal(
            barrier, inc=1, device_id={"ctx": lax.rem(me + k, n)}, device_id_type=MESH
        )
    for k in range(1, n_grp):
        pl.semaphore_signal(
            barrier, inc=1, device_id={"grp": lax.rem(my_grp + k, n_grp)}, device_id_type=MESH
        )
    pl.semaphore_wait(barrier, n - 1 + n_grp - 1)

    def target_at(k):
        return jnp.bitwise_xor(me, k) if n & (n - 1) == 0 else lax.rem(me + k, n)

    def source_at(k):
        return jnp.bitwise_xor(me, k) if n & (n - 1) == 0 else lax.rem(me - k + n, n)

    spans = ((rows - flen, flen), (0, rows - flen))

    def stream_copy(p, target, source):
        first, size = spans[p]
        start = pl.multiple_of(flen + source * rows + first, flen)
        return pltpu.make_async_remote_copy(
            src_ref=streams.at[:, pl.ds(first, size), col_of(target)],
            dst_ref=buf.at[:, pl.ds(start, size), :],
            send_sem=send_sem.at[target, p],
            recv_sem=recv_sem.at[source, p],
            device_id={"ctx": target},
            device_id_type=MESH,
        )

    def own_copy():
        return pltpu.make_async_copy(
            streams.at[:, :, col_of(me)], buf.at[:, row_of(me), :], local_sem.at[0]
        )

    own_copy().start()
    for p in range(2):
        for k in range(1, n):
            stream_copy(p, target_at(k), me).start()

    for s in range(3):
        buf[s, pl.ds(0, flen), :] = jnp.zeros((flen, cols), buf.dtype)
    taps[...] = filters[...].astype(jnp.float32)
    row_id = lax.broadcasted_iota(jnp.int32, (flen, flen), 0)
    col_id = lax.broadcasted_iota(jnp.int32, (flen, flen), 1)

    @pl.loop(0, 3 * own_groups)
    def _(idx):
        s = idx // own_groups
        g = lax.rem(idx, own_groups)
        line = taps[s, pl.ds(me * own_groups + g, 1), :]
        turned = pltpu.roll(
            jnp.broadcast_to(line, (flen, flen)), 0, 1, stride=1, stride_axis=0
        ).T
        lower = jnp.where(col_id <= row_id, turned, 0.0)
        upper = jnp.where(col_id > row_id, turned, 0.0)
        where = pl.ds(pl.multiple_of(g * flen, flen), flen)
        toep[s, where, pl.ds(0, flen)] = upper.astype(toep.dtype)
        toep[s, where, pl.ds(flen, flen)] = lower.astype(toep.dtype)

    blocks = rows // flen
    lane_group = lax.broadcasted_iota(jnp.int32, (flen, blocks * LANES), 1)
    lane_group = lax.rem(lane_group, LANES) // width
    factor = HD ** (-0.5) * math.log2(math.e)

    def fold(values, op):
        result = values[:, :LANES]
        for c in range(1, values.shape[1] // LANES):
            result = op(result, values[:, c * LANES : (c + 1) * LANES])
        return result

    def filter_block(i):
        @pl.loop(0, 3)
        def _(s):
            for h in range(heads):
                lanes = pl.ds(h * LANES, LANES)
                window = [
                    buf[s, pl.ds(pl.multiple_of(i * rows + b * flen, flen), 2 * flen), lanes]
                    for b in range(blocks)
                ]
                matrix = toep[s, pl.ds(h * per_tile * flen, per_tile * flen), :]
                product = jnp.dot(
                    matrix, jnp.concatenate(window, axis=1), preferred_element_type=jnp.float32
                )
                result = product[:flen]
                for g in range(1, per_tile):
                    result = jnp.where(
                        lane_group == g, product[g * flen : (g + 1) * flen], result
                    )
                result = result.astype(feat.dtype)
                for b in range(blocks):
                    feat[
                        s, pl.ds(pl.multiple_of(i * rows + b * flen, flen), flen), lanes
                    ] = result[:, b * LANES : (b + 1) * LANES]

    def rows_at(j):
        return pl.ds(pl.multiple_of(j * rows, flen), rows)

    def score(q, key, h):
        lanes = pl.ds(h * HD, HD)
        return lax.dot_general(
            feat[0, rows_at(q), lanes],
            feat[1, rows_at(key), lanes],
            (((1,), (1,)), ((), ())),
            preferred_element_type=jnp.float32,
        )

    def mixed(weights, key, h):
        return jnp.dot(
            weights.astype(jnp.bfloat16),
            feat[2, rows_at(key), pl.ds(h * HD, HD)],
            preferred_element_type=jnp.float32,
        )

    def open_block(q, h):
        place = lax.broadcasted_iota(jnp.int32, (rows, rows), 0)
        other = lax.broadcasted_iota(jnp.int32, (rows, rows), 1)
        block = jnp.where(other <= place, score(q, q, h), -1e30)
        new = jnp.max(fold(block, jnp.maximum), axis=1, keepdims=True)
        weights = jnp.exp2((block - new) * factor)
        at = q * heads + h
        top[at] = jnp.broadcast_to(new, (rows, LANES))
        total[at] = fold(weights, jnp.add)
        accum[at] = mixed(weights, q, h)

    def add_block(q, key, h):
        at = q * heads + h
        block = score(q, key, h)
        old = top[at]
        new = jnp.maximum(old, jnp.max(fold(block, jnp.maximum), axis=1, keepdims=True))
        shrink = jnp.exp2((old - new) * factor)
        weights = jnp.exp2((block - new[:, :1]) * factor)
        top[at] = new
        total[at] = total[at] * shrink + fold(weights, jnp.add)
        accum[at] = accum[at] * shrink + mixed(weights, key, h)

    def close_block(q, h):
        at = q * heads + h
        sum_of = jnp.sum(total[at], axis=1, keepdims=True)
        return (accum[at] / sum_of).astype(jnp.bfloat16)

    def back_copy(target, source):
        return pltpu.make_async_remote_copy(
            src_ref=sending.at[target],
            dst_ref=att.at[:, col_of(source)],
            send_sem=back_send.at[target],
            recv_sem=back_recv.at[source],
            device_id={"ctx": target},
            device_id_type=MESH,
        )

    for k in range(1, n):
        source = source_at(k)
        stream_copy(0, source, source).wait_recv()
    own_copy().wait()

    @pl.loop(0, n)
    def _(k):
        b = source_at(k)

        @pl.when(k > 0)
        def _():
            stream_copy(1, b, b).wait_recv()

        filter_block(b)
        for h in range(heads):
            open_block(b, h)

            @pl.loop(0, k)
            def _(before):
                o = source_at(before)
                add_block(jnp.maximum(b, o), jnp.minimum(b, o), h)

    @pl.loop(0, n)
    def _(k):
        i = source_at(k)
        for h in range(heads):
            sending[i, :, pl.ds(h * HD, HD)] = close_block(i, h)

        @pl.when(i != me)
        def _():
            back_copy(i, me).start()

        @pl.when(i == me)
        def _():
            att[:, col_of(me)] = sending[i]

    for k in range(1, n):
        source = lax.rem(me + k, n)
        back_copy(source, source).wait_recv()

    @pl.loop(0, blocks)
    def _(b):
        part = pl.ds(pl.multiple_of(b * flen, flen), flen)
        wide = att[part, :].astype(jnp.float32)
        squares = fold(wide * wide, jnp.add).T
        squares = squares.reshape(LANES // 8, 8, flen)
        sums[0, :, part] = jnp.sum(squares, axis=0)

    def sum_copy(k, turn):
        return pltpu.make_async_remote_copy(
            src_ref=sums.at[0],
            dst_ref=sums.at[k],
            send_sem=sum_send.at[k],
            recv_sem=sum_recv.at[k],
            device_id={"grp": lax.rem(my_grp + turn, n_grp)},
            device_id_type=MESH,
        )

    for k in range(1, n_grp):
        sum_copy(k, k).start()
    for k in range(1, n_grp):
        sum_copy(k, k).wait()

    @pl.loop(0, blocks)
    def _(b):
        part = pl.ds(pl.multiple_of(b * flen, flen), flen)
        power = sums[0, :, part]
        for k in range(1, n_grp):
            power = power + sums[k, :, part]
        power = jnp.sum(power, axis=0, keepdims=True) / (chans * n_grp)
        power = jnp.broadcast_to(lax.rsqrt(power + 1e-06), (LANES, flen)).T
        wide = att[part, :].astype(jnp.float32)
        for c in range(chans // LANES):
            lanes = slice(c * LANES, (c + 1) * LANES)
            out[part, lanes] = (wide[:, lanes] * gain[:, lanes] * power).astype(out.dtype)

    for k in range(1, n):
        target = lax.rem(me + k, n)
        for p in range(2):
            stream_copy(p, target, me).wait_send()
        back_copy(target, me).wait_send()


def fused(streams, filters, gain):
    n, n_grp = lax.axis_size("ctx"), lax.axis_size("grp")
    _, rows, chans = streams.shape
    _, groups, flen = filters.shape
    cols = chans // n
    tokens = rows * n
    vmem = pl.BlockSpec(memory_space=pltpu.VMEM)
    return pl.pallas_call(
        functools.partial(fused_kernel, n, n_grp),
        out_shape=jax.ShapeDtypeStruct((rows, chans), jnp.bfloat16),
        in_specs=[pl.BlockSpec(memory_space=pl.ANY), vmem, vmem],
        out_specs=vmem,
        scratch_shapes=[
            pltpu.VMEM((3, flen + tokens, cols), jnp.bfloat16),
            pltpu.VMEM((3, groups, flen), jnp.float32),
            pltpu.VMEM((3, groups // n * flen, 2 * flen), jnp.bfloat16),
            pltpu.VMEM((3, tokens, cols), jnp.bfloat16),
            pltpu.VMEM((chans // HD, rows, LANES), jnp.float32),
            pltpu.VMEM((chans // HD, rows, LANES), jnp.float32),
            pltpu.VMEM((chans // HD, rows, HD), jnp.float32),
            pltpu.VMEM((n, rows, cols), jnp.bfloat16),
            pltpu.VMEM((rows, chans), jnp.bfloat16),
            pltpu.VMEM((n_grp, 8, rows), jnp.float32),
            pltpu.SemaphoreType.DMA((1,)),
            pltpu.SemaphoreType.DMA((n, 2)),
            pltpu.SemaphoreType.DMA((n, 2)),
            pltpu.SemaphoreType.DMA((n,)),
            pltpu.SemaphoreType.DMA((n,)),
            pltpu.SemaphoreType.DMA((n_grp,)),
            pltpu.SemaphoreType.DMA((n_grp,)),
        ],
        compiler_params=pltpu.CompilerParams(collective_id=0, has_side_effects=True),
        name="fused",
    )(streams, filters, gain.reshape(1, chans))


def passed_along(block, axis, distance):
    devices = range(lax.axis_size(axis))
    route = [(i - distance, i) for i in devices if i - distance in devices]
    return lax.ppermute(block, axis, route)


def filter_all(streams, filters):
    tok_rows = streams.shape[1]
    chan_count = streams.shape[2]
    filt_len = filters.shape[2]
    group_count = filters.shape[1]
    group_width = chan_count // group_count
    tail = streams[:, tok_rows - filt_len :, :]
    before = passed_along(tail, "ctx", 1)
    padded = jnp.concatenate([before, streams], axis=1)
    block_count = tok_rows // filt_len
    blocks = padded.reshape(3, block_count + 1, filt_len, group_count, group_width)
    lag_table = np.arange(filt_len)[:, None] - np.arange(filt_len)[None, :]
    lower_idx = np.where(lag_table >= 0, lag_table, 0)
    upper_idx = np.where(lag_table < 0, lag_table + filt_len, 0)
    lower = jnp.where(lag_table >= 0, filters[:, :, lower_idx], 0.0)
    upper = jnp.where(lag_table < 0, filters[:, :, upper_idx], 0.0)
    result = jnp.einsum(
        "agts,absgc->abtgc", lower, blocks[:, 1:], preferred_element_type=jnp.float32
    )
    result = result + jnp.einsum(
        "agts,absgc->abtgc", upper, blocks[:, :-1], preferred_element_type=jnp.float32
    )
    return result.reshape(3, tok_rows, chan_count).astype(jnp.bfloat16)


def attend(queries, positions, keyed, valued):
    tok_rows, chan_count = queries.shape
    head_count = chan_count // HD
    scale = HD ** (-0.5)
    query_heads = queries.reshape(tok_rows, head_count, HD)
    query_last = jnp.max(positions)
    start_state = (
        jnp.full((head_count, tok_rows), -1e30, jnp.float32),
        jnp.zeros((head_count, tok_rows), jnp.float32),
        jnp.zeros((tok_rows, head_count, HD), jnp.float32),
    )
    key_piece = lax.all_gather(keyed, "ctx", axis=0, tiled=True)
    value_piece = lax.all_gather(valued, "ctx", axis=0, tiled=True)
    piece_len = key_piece.shape[0]
    block_len = math.gcd(piece_len, 512)

    def step_block(step_idx, state):
        offset = step_idx * block_len
        key_block = lax.dynamic_slice_in_dim(key_piece, offset, block_len, 0).reshape(
            block_len, head_count, HD
        )
        value_block = lax.dynamic_slice_in_dim(value_piece, offset, block_len, 0).reshape(
            block_len, head_count, HD
        )
        key_pos = offset + jnp.arange(block_len, dtype=jnp.int32)

        def update_block(inner):
            running, totals, accum = inner
            scores = (
                jnp.einsum(
                    "shd,khd->hsk", query_heads, key_block, preferred_element_type=jnp.float32
                )
                * scale
            )
            causal = key_pos[None, None, :] <= positions[None, :, None]
            newtop = jnp.maximum(running, jnp.max(jnp.where(causal, scores, -1e30), axis=2))
            weights = jnp.where(causal, jnp.exp(scores - newtop[:, :, None]), 0.0)
            factor = jnp.exp(running - newtop)
            totals = totals * factor + jnp.sum(weights, axis=2)
            accum = accum * factor.T[:, :, None] + jnp.einsum(
                "hsk,khd->shd",
                weights.astype(jnp.bfloat16),
                value_block,
                preferred_element_type=jnp.float32,
            )
            return (newtop, totals, accum)

        return lax.cond(offset > query_last, lambda inner: inner, update_block, state)

    running, totals, accum = lax.fori_loop(0, piece_len // block_len, step_block, start_state)
    return (accum / totals.T[:, :, None]).reshape(tok_rows, chan_count).astype(jnp.bfloat16)


def local(streams, filters, gain):
    features = filter_all(streams, filters)
    tok_rows = streams.shape[1]
    my_index = lax.axis_index("ctx")
    queries = features[0]
    positions = my_index * tok_rows + jnp.arange(tok_rows, dtype=jnp.int32)
    attended = attend(queries, positions, features[1], features[2])
    wide = attended.astype(jnp.float32)
    power = lax.psum(jnp.sum(wide * wide, axis=1), "grp") / (streams.shape[2] * lax.axis_size("grp"))
    return (wide * gain[None, :] * lax.rsqrt(power + 1e-06)[:, None]).astype(jnp.bfloat16)


def chosen(streams, filters, gain):
    n = lax.axis_size("ctx")
    _, rows, chans = streams.shape
    _, groups, flen = filters.shape
    whole_heads = chans % (n * HD) == 0
    fits = flen == LANES and rows % flen == 0 and LANES % (chans // groups) == 0
    if n > 1 and whole_heads and fits and groups % n == 0:
        return fused(streams, filters, gain)
    return local(streams, filters, gain)


def solution(mesh):
    placed = (P(None, "ctx", "grp"), P(None, "grp", None), P("grp"))
    return jax.shard_map(
        chosen, mesh=mesh, in_specs=placed, out_specs=P("ctx", "grp"), check_vma=False
    )
```

profile of v0, /device:TPU:0, one launch (start us, length us, event | category | flops | bytes accessed | tf_op | source)
XLA Modules:
  0.0 92.3 jit_solution(12943567177725373717)
XLA Ops:
  0.0 90.2 %fused.1 = bf16[384,1024]{1,0:T(8,128)(2,1)} custom-call(bf16[3,384,1024]{2,1,0:T(8,128)(2,1)} %streams.1, bf16[3,64,128]{2,1,0:T(8,128)(2,1)} %filters.1, f32[1,1024]{1,0:T(1,128)} %bitcast.1), custom_call_target="tpu_custom_call" | custom-call | tf_op jit(solution)/shard_map/fused/pallas_call | solution.py:302
  90.2 2.1 %copy.5 = bf16[384,1024]{1,0:T(8,128)(2,1)} copy(bf16[384,1024]{1,0:T(8,128)(2,1)} %fused.1) | data formatting | bytes 1572864
where the time goes:
time: 92.5 us; the launch traced here: 92.3 us
  Pallas kernels  90.2 us (98%)
  local copies, waits for them, and re-layouts  2.06 us (2%)
    pallas_call x1, Pallas kernels, fused(): pl.pallas_call(functools.partial(fused_kernel, n, n_grp), out_shape=jax.S...  90.2 us
    unnamed x1, local copies, waits for them, and re-layouts  2.06 us

commit v1 on v0

v1 whole, which is shorter than its diff:
```python
import functools
import math

import jax
import jax.numpy as jnp
import numpy as np
from jax import lax
from jax.experimental import pallas as pl
from jax.experimental.pallas import tpu as pltpu
from jax.sharding import PartitionSpec as P

HD = 128
LANES = 128
MESH = pl.DeviceIdType.MESH
SIDES = 2
LAYERS = 4
HUB = 1


def layered_kernel(
    n,
    n_grp,
    streams,
    filters,
    gain,
    out,
    buf,
    turned,
    toep,
    feat,
    far_kv,
    far_q,
    part,
    part_stat,
    inbox,
    in_stat,
    own_acc,
    own_top,
    own_total,
    sending,
    att,
    sums,
    local_sem,
    side_send,
    side_recv,
    halo_send,
    halo_recv,
    kv_send,
    kv_recv,
    q_send,
    q_recv,
    part_send,
    part_recv,
    stat_send,
    stat_recv,
    back_send,
    back_recv,
    sum_send,
    sum_recv,
):
    me = lax.axis_index("ctx")
    my_grp = lax.axis_index("grp")
    layer = me // SIDES
    side = lax.rem(me, SIDES)
    other = 1 - side
    rows = streams.shape[1]
    chans = streams.shape[2]
    groups = filters.shape[1]
    flen = filters.shape[2]
    half = chans // SIDES
    heads = half // HD
    span = rows * SIDES
    width = chans // groups
    per_tile = LANES // width
    factor = HD ** (-0.5) * math.log2(math.e)

    def place(z, y):
        return {"ctx": z * SIDES + y}

    def lanes_of(h):
        return pl.ds(pl.multiple_of(h * HD, HD), HD)

    def half_lanes(y, h):
        return pl.ds(pl.multiple_of(y * half + h * HD, HD), HD)

    def remote(src, dst, send, recv, device):
        return pltpu.make_async_remote_copy(
            src_ref=src,
            dst_ref=dst,
            send_sem=send,
            recv_sem=recv,
            device_id=device,
            device_id_type=MESH,
        )

    def own_copy():
        start = pl.multiple_of(flen + side * rows, flen)
        return pltpu.make_async_copy(
            streams.at[:, :, pl.ds(pl.multiple_of(side * half, HD), half)],
            buf.at[:, pl.ds(start, rows), :],
            local_sem.at[0],
        )

    def side_copy(s, h, y):
        start = pl.multiple_of(flen + y * rows, flen)
        return remote(
            streams.at[s, :, half_lanes(1 - y, h)],
            buf.at[s, pl.ds(start, rows), lanes_of(h)],
            side_send.at[s, h],
            side_recv.at[s, h],
            place(layer, other),
        )

    def halo_copy(h, y):
        return remote(
            streams.at[:, pl.ds(rows - flen, flen), half_lanes(y, h)],
            buf.at[:, pl.ds(0, flen), lanes_of(h)],
            halo_send.at[y, h],
            halo_recv.at[h],
            place(lax.rem(layer + 1, LAYERS), y),
        )

    def kv_copy(h):
        return remote(
            feat.at[pl.ds(1, 2), :, lanes_of(h)],
            far_kv.at[:, :, lanes_of(h)],
            kv_send.at[h],
            kv_recv.at[h],
            place(HUB, side),
        )

    def q_copy(d, h):
        return remote(
            feat.at[0, :, lanes_of(h)],
            far_q.at[d, :, lanes_of(h)],
            q_send.at[d, h],
            q_recv.at[d, h],
            place(lax.rem(layer + LAYERS - d - 1, LAYERS), side),
        )

    def part_copy(d, h, r):
        where = pl.ds(r * rows, rows)
        return remote(
            part.at[d, where, lanes_of(h)],
            inbox.at[d, where, lanes_of(h)],
            part_send.at[d, h, r],
            part_recv.at[d, h, r],
            place(lax.rem(layer + d + 1, LAYERS), side),
        )

    def stat_copy(d, h, r):
        return remote(
            part_stat.at[d, h, r],
            in_stat.at[d, h, r],
            stat_send.at[d, h, r],
            stat_recv.at[d, h, r],
            place(lax.rem(layer + d + 1, LAYERS), side),
        )

    def back_copy(h, y):
        return remote(
            sending.at[:, lanes_of(h)],
            att.at[:, half_lanes(y, h)],
            back_send.at[h],
            back_recv.at[h],
            place(layer, other),
        )

    barrier = pltpu.get_barrier_semaphore()
    for k in range(1, n):
        pl.semaphore_signal(
            barrier, inc=1, device_id={"ctx": lax.rem(me + k, n)}, device_id_type=MESH
        )
    for k in range(1, n_grp):
        pl.semaphore_signal(
            barrier, inc=1, device_id={"grp": lax.rem(my_grp + k, n_grp)}, device_id_type=MESH
        )
    own_copy().start()
    pl.semaphore_wait(barrier, n - 1 + n_grp - 1)

    lead = jnp.where(layer <= HUB, 1, 0)

    def stream_at(j):
        return lax.rem(j + lead, 3)

    @pl.loop(0, heads)
    def _(h):
        for j in range(3):
            side_copy(stream_at(j), h, side).start()

        @pl.when((side == SIDES - 1) & (layer < LAYERS - 1))
        def _():
            for y in range(SIDES):
                halo_copy(h, y).start()

    @pl.when(layer == 0)
    def _():
        for s in range(3):
            buf[s, pl.ds(0, flen), :] = jnp.zeros((flen, half), buf.dtype)

    own_groups = half // width
    row_id = lax.broadcasted_iota(jnp.int32, (flen, flen), 0)
    col_id = lax.broadcasted_iota(jnp.int32, (flen, flen), 1)
    flip = jnp.where(
        (row_id + col_id == flen) | ((row_id == 0) & (col_id == 0)), 1.0, 0.0
    ).astype(jnp.bfloat16)
    for s in range(3):
        turned[s] = jnp.dot(
            filters[s, pl.ds(pl.multiple_of(side * own_groups, own_groups), own_groups), :],
            flip,
            preferred_element_type=jnp.float32,
        )

    def build(h):
        @pl.loop(0, 3)
        def _(s):
            lines = turned[s, pl.ds(pl.multiple_of(h * per_tile, per_tile), per_tile), :]
            for g in range(per_tile):
                table = pltpu.roll(
                    jnp.broadcast_to(lines[g : g + 1], (flen, flen)),
                    0,
                    1,
                    stride=1,
                    stride_axis=0,
                )
                lower = jnp.where(col_id <= row_id, table, 0.0)
                upper = jnp.where(col_id > row_id, table, 0.0)
                where = pl.ds(g * flen, flen)
                toep[s, where, pl.ds(0, flen)] = upper.astype(toep.dtype)
                toep[s, where, pl.ds(flen, flen)] = lower.astype(toep.dtype)

    blocks = span // flen
    lane_group = lax.broadcasted_iota(jnp.int32, (flen, blocks * LANES), 1)
    lane_group = lax.rem(lane_group, LANES) // width

    def fold(values, op):
        result = values[:, :LANES]
        for c in range(1, values.shape[1] // LANES):
            result = op(result, values[:, c * LANES : (c + 1) * LANES])
        return result

    def filter_head(s, h):
        lanes = lanes_of(h)
        window = [buf[s, pl.ds(b * flen, 2 * flen), lanes] for b in range(blocks)]
        product = jnp.dot(
            toep[s], jnp.concatenate(window, axis=1), preferred_element_type=jnp.float32
        )
        result = product[:flen]
        for g in range(1, per_tile):
            result = jnp.where(lane_group == g, product[g * flen : (g + 1) * flen], result)
        result = result.astype(feat.dtype)
        for b in range(blocks):
            feat[s, pl.ds(b * flen, flen), lanes] = result[:, b * LANES : (b + 1) * LANES]

    def attend(query, pieces):
        parts = []
        for key, _, last in pieces:
            block = lax.dot_general(
                query, key, (((1,), (1,)), ((), ())), preferred_element_type=jnp.float32
            )
            if last:
                line = lax.broadcasted_iota(jnp.int32, block.shape, 0)
                spot = lax.broadcasted_iota(jnp.int32, block.shape, 1)
                block = jnp.where(spot <= line, block, -1e30)
            parts.append(block)
        top = functools.reduce(jnp.maximum, [fold(p, jnp.maximum) for p in parts])
        top = jnp.max(top, axis=1, keepdims=True)
        weights = [jnp.exp2((p - top) * factor) for p in parts]
        total = functools.reduce(jnp.add, [fold(w, jnp.add) for w in weights])
        total = jnp.sum(total, axis=1, keepdims=True)
        mixed = [
            jnp.dot(w.astype(jnp.bfloat16), p[1], preferred_element_type=jnp.float32)
            for w, p in zip(weights, pieces)
        ]
        return functools.reduce(jnp.add, mixed), top, total

    def piece(ref, base, h, first, size, last=False):
        where = pl.ds(first, size)
        return (ref[base, where, lanes_of(h)], ref[base + 1, where, lanes_of(h)], last)

    def own_pieces(h, r):
        before = [piece(feat, 1, h, 0, r * rows)] if r else []
        return before + [piece(feat, 1, h, r * rows, rows, True)]

    def query_of(h, r):
        return feat[0, pl.ds(r * rows, rows), lanes_of(h)]

    def finish(h, r, values):
        @pl.when(side == r)
        def _():
            att[:, half_lanes(side, h)] = values

        @pl.when(side != r)
        def _():
            sending[:, lanes_of(h)] = values

    lane_id = lax.broadcasted_iota(jnp.int32, (rows, LANES), 1)

    def serve(d, h, pieces):
        q_copy(d, h).wait_recv()
        results = [
            attend(far_q[d, pl.ds(r * rows, rows), lanes_of(h)], pieces) for r in range(SIDES)
        ]
        for r, (mixed, top, total) in enumerate(results):
            part[d, pl.ds(r * rows, rows), lanes_of(h)] = (mixed / total).astype(part.dtype)
            stat = jnp.where(lane_id == 0, top, total)
            part_stat[d, h, r] = stat.T[:8]
        for r in range(SIDES):
            part_copy(d, h, r).start()
            stat_copy(d, h, r).start()

    def keep(h):
        for r in range(SIDES):
            mixed, top, total = attend(query_of(h, r), own_pieces(h, r))
            own_acc[h, r] = mixed
            own_top[h, r] = jnp.broadcast_to(top, (rows, LANES))
            own_total[h, r] = jnp.broadcast_to(total, (rows, LANES))

    def spread(line):
        return jnp.broadcast_to(line, (LANES, rows)).T

    def merge(h, count):
        for r in range(SIDES):
            for d in range(count):
                part_copy(d, h, r).wait_recv()
                stat_copy(d, h, r).wait_recv()
        for r in range(SIDES):
            where = pl.ds(r * rows, rows)
            tops = [own_top[h, r]] + [spread(in_stat[d, h, r, 0:1, :]) for d in range(count)]
            totals = [own_total[h, r]] + [spread(in_stat[d, h, r, 1:2, :]) for d in range(count)]
            top = functools.reduce(jnp.maximum, tops)
            scales = [jnp.exp2((t - top) * factor) for t in tops]
            total = functools.reduce(jnp.add, [a * b for a, b in zip(scales, totals)])
            mixed = own_acc[h, r] * scales[0]
            for d in range(count):
                values = inbox[d, where, lanes_of(h)].astype(jnp.float32)
                mixed = mixed + values * (scales[d + 1] * totals[d + 1])
            finish(h, r, (mixed / total).astype(jnp.bfloat16))
        back_copy(h, side).start()

    @pl.loop(0, heads)
    def _(h):
        build(h)

        @pl.when(h == 0)
        def _():
            own_copy().wait()

        @pl.when(layer > 0)
        def _():
            halo_copy(h, 0).wait_recv()

        @pl.loop(0, 3)
        def _(j):
            s = stream_at(j)
            side_copy(s, h, side).wait_recv()
            filter_head(s, h)

            @pl.when((layer == 0) & (j == 1))
            def _():
                kv_copy(h).start()

            @pl.when((layer == LAYERS - 1) & (j == 0))
            def _():
                q_copy(1, h).start()

            @pl.when((layer > HUB) & (j == 0))
            def _():
                q_copy(0, h).start()

        @pl.when(layer == 0)
        def _():
            for r in range(SIDES):
                mixed, _, total = attend(query_of(h, r), own_pieces(h, r))
                finish(h, r, (mixed / total).astype(jnp.bfloat16))
            back_copy(h, side).start()

        @pl.when(layer == HUB)
        def _():
            kv_copy(h).wait_recv()
            far = piece(far_kv, 0, h, 0, span)
            for r in range(SIDES):
                mixed, _, total = attend(query_of(h, r), [far] + own_pieces(h, r))
                finish(h, r, (mixed / total).astype(jnp.bfloat16))
            back_copy(h, side).start()

            @pl.loop(0, LAYERS - 1 - HUB)
            def _(d):
                serve(d, h, [piece(far_kv, 0, h, 0, span), piece(feat, 1, h, 0, span)])

        @pl.when(layer > HUB)
        def _():
            keep(h)

        @pl.when((layer > HUB) & (layer < LAYERS - 1))
        def _():
            serve(0, h, [piece(feat, 1, h, 0, span)])

    @pl.when(layer == LAYERS - 2)
    def _():
        @pl.loop(0, heads)
        def _(h):
            merge(h, 1)

    @pl.when(layer == LAYERS - 1)
    def _():
        @pl.loop(0, heads)
        def _(h):
            merge(h, 2)

    @pl.loop(0, heads)
    def _(h):
        back_copy(h, side).wait_recv()

    row_blocks = rows // flen

    @pl.loop(0, row_blocks)
    def _(b):
        where = pl.ds(pl.multiple_of(b * flen, flen), flen)
        wide = att[where, :].astype(jnp.float32)
        squares = fold(wide * wide, jnp.add).T
        squares = squares.reshape(LANES // 8, 8, flen)
        sums[0, :, where] = jnp.sum(squares, axis=0)

    def sum_copy(k):
        return remote(
            sums.at[0],
            sums.at[k],
            sum_send.at[k],
            sum_recv.at[k],
            {"grp": lax.rem(my_grp + k, n_grp)},
        )

    for k in range(1, n_grp):
        sum_copy(k).start()
    for k in range(1, n_grp):
        sum_copy(k).wait()

    @pl.loop(0, row_blocks)
    def _(b):
        where = pl.ds(pl.multiple_of(b * flen, flen), flen)
        power = sums[0, :, where]
        for k in range(1, n_grp):
            power = power + sums[k, :, where]
        power = jnp.sum(power, axis=0, keepdims=True) / (chans * n_grp)
        power = jnp.broadcast_to(lax.rsqrt(power + 1e-06), (LANES, flen)).T
        wide = att[where, :].astype(jnp.float32)
        for c in range(chans // LANES):
            lanes = slice(c * LANES, (c + 1) * LANES)
            out[where, lanes] = (wide[:, lanes] * gain[:, lanes] * power).astype(out.dtype)

    @pl.loop(0, heads)
    def _(h):
        for s in range(3):
            side_copy(s, h, side).wait_send()
        back_copy(h, side).wait_send()

        @pl.when((side == SIDES - 1) & (layer < LAYERS - 1))
        def _():
            for y in range(SIDES):
                halo_copy(h, y).wait_send()

        @pl.when(layer == 0)
        def _():
            kv_copy(h).wait_send()

        @pl.when(layer > HUB)
        def _():
            q_copy(0, h).wait_send()

        @pl.when(layer == LAYERS - 1)
        def _():
            q_copy(1, h).wait_send()

        @pl.when((layer >= HUB) & (layer < LAYERS - 1))
        def _():
            for r in range(SIDES):
                part_copy(0, h, r).wait_send()
                stat_copy(0, h, r).wait_send()

        @pl.when(layer == HUB)
        def _():
            for r in range(SIDES):
                part_copy(1, h, r).wait_send()
                stat_copy(1, h, r).wait_send()


def layered(streams, filters, gain):
    n, n_grp = lax.axis_size("ctx"), lax.axis_size("grp")
    _, rows, chans = streams.shape
    _, groups, flen = filters.shape
    half = chans // SIDES
    heads = half // HD
    span = rows * SIDES
    per_tile = LANES * groups // chans
    vmem = pl.BlockSpec(memory_space=pltpu.VMEM)
    dma = pltpu.SemaphoreType.DMA
    low = jnp.bfloat16
    far = LAYERS - 1 - HUB
    return pl.pallas_call(
        functools.partial(layered_kernel, n, n_grp),
        out_shape=jax.ShapeDtypeStruct((rows, chans), low),
        in_specs=[pl.BlockSpec(memory_space=pl.ANY), vmem, vmem],
        out_specs=vmem,
        scratch_shapes=[
            pltpu.VMEM((3, flen + span, half), low),
            pltpu.VMEM((3, groups // SIDES, flen), jnp.float32),
            pltpu.VMEM((3, per_tile * flen, 2 * flen), low),
            pltpu.VMEM((3, span, half), low),
            pltpu.VMEM((2, span, half), low),
            pltpu.VMEM((far, span, half), low),
            pltpu.VMEM((far, span, half), low),
            pltpu.VMEM((far, heads, SIDES, 8, rows), jnp.float32),
            pltpu.VMEM((far, span, half), low),
            pltpu.VMEM((far, heads, SIDES, 8, rows), jnp.float32),
            pltpu.VMEM((heads, SIDES, rows, HD), jnp.float32),
            pltpu.VMEM((heads, SIDES, rows, LANES), jnp.float32),
            pltpu.VMEM((heads, SIDES, rows, LANES), jnp.float32),
            pltpu.VMEM((rows, half), low),
            pltpu.VMEM((rows, chans), low),
            pltpu.VMEM((n_grp, 8, rows), jnp.float32),
            dma((1,)),
            dma((3, heads)),
            dma((3, heads)),
            dma((SIDES, heads)),
            dma((heads,)),
            dma((heads,)),
            dma((heads,)),
            dma((far, heads)),
            dma((far, heads)),
            dma((far, heads, SIDES)),
            dma((far, heads, SIDES)),
            dma((far, heads, SIDES)),
            dma((far, heads, SIDES)),
            dma((heads,)),
            dma((heads,)),
            dma((n_grp,)),
            dma((n_grp,)),
        ],
        compiler_params=pltpu.CompilerParams(
            collective_id=0, has_side_effects=True, vmem_limit_bytes=56 * 2**20
        ),
        name="layered",
    )(streams, filters, gain.reshape(1, chans))


def passed_along(block, axis, distance):
    devices = range(lax.axis_size(axis))
    route = [(i - distance, i) for i in devices if i - distance in devices]
    return lax.ppermute(block, axis, route)


def filter_all(streams, filters):
    tok_rows = streams.shape[1]
    chan_count = streams.shape[2]
    filt_len = filters.shape[2]
    group_count = filters.shape[1]
    group_width = chan_count // group_count
    tail = streams[:, tok_rows - filt_len :, :]
    before = passed_along(tail, "ctx", 1)
    padded = jnp.concatenate([before, streams], axis=1)
    block_count = tok_rows // filt_len
    blocks = padded.reshape(3, block_count + 1, filt_len, group_count, group_width)
    zeros = jnp.zeros_like(filters)
    line = jnp.concatenate([zeros[..., :1], filters[..., ::-1], zeros], axis=2)
    table = jnp.broadcast_to(line[:, :, None, :], line.shape[:2] + (filt_len, line.shape[2]))
    table = table.reshape(3, group_count, -1)[..., : 2 * filt_len * filt_len]
    table = table.reshape(3, group_count, filt_len, 2 * filt_len)
    upper, lower = table[..., :filt_len], table[..., filt_len:]
    result = jnp.einsum(
        "agts,absgc->abtgc", lower, blocks[:, 1:], preferred_element_type=jnp.float32
    )
    result = result + jnp.einsum(
        "agts,absgc->abtgc", upper, blocks[:, :-1], preferred_element_type=jnp.float32
    )
    return result.reshape(3, tok_rows, chan_count).astype(jnp.bfloat16)


def attend(queries, positions, keyed, valued):
    tok_rows, chan_count = queries.shape
    head_count = chan_count // HD
    scale = HD ** (-0.5)
    query_heads = queries.reshape(tok_rows, head_count, HD)
    query_last = jnp.max(positions)
    start_state = (
        jnp.full((head_count, tok_rows), -1e30, jnp.float32),
        jnp.zeros((head_count, tok_rows), jnp.float32),
        jnp.zeros((tok_rows, head_count, HD), jnp.float32),
    )
    key_piece = lax.all_gather(keyed, "ctx", axis=0, tiled=True)
    value_piece = lax.all_gather(valued, "ctx", axis=0, tiled=True)
    piece_len = key_piece.shape[0]
    block_len = math.gcd(piece_len, 512)

    def step_block(step_idx, state):
        offset = step_idx * block_len
        key_block = lax.dynamic_slice_in_dim(key_piece, offset, block_len, 0).reshape(
            block_len, head_count, HD
        )
        value_block = lax.dynamic_slice_in_dim(value_piece, offset, block_len, 0).reshape(
            block_len, head_count, HD
        )
        key_pos = offset + jnp.arange(block_len, dtype=jnp.int32)

        def update_block(inner):
            running, totals, accum = inner
            scores = (
                jnp.einsum(
                    "shd,khd->hsk", query_heads, key_block, preferred_element_type=jnp.float32
                )
                * scale
            )
            causal = key_pos[None, None, :] <= positions[None, :, None]
            newtop = jnp.maximum(running, jnp.max(jnp.where(causal, scores, -1e30), axis=2))
            weights = jnp.where(causal, jnp.exp(scores - newtop[:, :, None]), 0.0)
            factor = jnp.exp(running - newtop)
            totals = totals * factor + jnp.sum(weights, axis=2)
            accum = accum * factor.T[:, :, None] + jnp.einsum(
                "hsk,khd->shd",
                weights.astype(jnp.bfloat16),
                value_block,
                preferred_element_type=jnp.float32,
            )
            return (newtop, totals, accum)

        return lax.cond(offset > query_last, lambda inner: inner, update_block, state)

    running, totals, accum = lax.fori_loop(0, piece_len // block_len, step_block, start_state)
    return (accum / totals.T[:, :, None]).reshape(tok_rows, chan_count).astype(jnp.bfloat16)


def local(streams, filters, gain):
    features = filter_all(streams, filters)
    tok_rows = streams.shape[1]
    my_index = lax.axis_index("ctx")
    queries = features[0]
    positions = my_index * tok_rows + jnp.arange(tok_rows, dtype=jnp.int32)
    attended = attend(queries, positions, features[1], features[2])
    wide = attended.astype(jnp.float32)
    power = lax.psum(jnp.sum(wide * wide, axis=1), "grp") / (streams.shape[2] * lax.axis_size("grp"))
    return (wide * gain[None, :] * lax.rsqrt(power + 1e-06)[:, None]).astype(jnp.bfloat16)


def chosen(streams, filters, gain):
    n = lax.axis_size("ctx")
    _, rows, chans = streams.shape
    _, groups, flen = filters.shape
    whole_heads = chans % (SIDES * HD) == 0
    fits = flen == LANES and rows % flen == 0 and LANES % (chans // groups) == 0
    if n == SIDES * LAYERS and whole_heads and fits:
        return layered(streams, filters, gain)
    return local(streams, filters, gain)


def solution(mesh):
    placed = (P(None, "ctx", "grp"), P(None, "grp", None), P("grp"))
    return jax.shard_map(
        chosen, mesh=mesh, in_specs=placed, out_specs=P("ctx", "grp"), check_vma=False
    )
```

time: 92.5 us -> 87.1 us (0.942)
  the two profiles are of different devices: /device:TPU:0 before, /device:TPU:25 now
where the time goes in v1:
time: 87.1 us; the launch traced here: 86.9 us
  Pallas kernels  84.8 us (97%)
  local copies, waits for them, and re-layouts  2.06 us (2%)
    pallas_call x1, Pallas kernels, layered(): pl.pallas_call(functools.partial(layered_kernel, n, n_grp), out_shape=jax...  84.8 us
    unnamed x1, local copies, waits for them, and re-layouts  2.06 us

profile of v1, /device:TPU:25, one launch (start us, length us, event | category | flops | bytes accessed | tf_op | source)
XLA Modules:
  0.0 86.9 jit_solution(10691612455092616969)
XLA Ops:
  0.0 84.8 %layered.1 = bf16[384,1024]{1,0:T(8,128)(2,1)} custom-call(bf16[3,384,1024]{2,1,0:T(8,128)(2,1)} %streams.1, bf16[3,64,128]{2,1,0:T(8,128)(2,1)} %filters.1, f32[1,1024]{1,0:T(1,128)} %bitcast.1), custom_call_target="tpu_custom_call" | custom-call | tf_op jit(solution)/shard_map/layered/pallas_call | solution.py:500
  84.8 2.1 %copy.5 = bf16[384,1024]{1,0:T(8,128)(2,1)} copy(bf16[384,1024]{1,0:T(8,128)(2,1)} %layered.1) | data formatting | bytes 1572864

commit v2 on v1

--- a/solution.py
+++ b/solution.py
@@ -101,31 +101,43 @@
             local_sem.at[0],
         )
 
-    def side_copy(s, h, y):
-        start = pl.multiple_of(flen + y * rows, flen)
-        return remote(
-            streams.at[s, :, half_lanes(1 - y, h)],
-            buf.at[s, pl.ds(start, rows), lanes_of(h)],
-            side_send.at[s, h],
-            side_recv.at[s, h],
+    spans = ((rows - flen, flen), (0, rows - flen))
+
+    def side_copy(s, h, p):
+        first, size = spans[p]
+        start = pl.multiple_of(flen + side * rows + first, flen)
+        return remote(
+            streams.at[s, pl.ds(first, size), half_lanes(other, h)],
+            buf.at[s, pl.ds(start, size), lanes_of(h)],
+            side_send.at[s, h, p],
+            side_recv.at[s, h, p],
             place(layer, other),
         )
 
-    def halo_copy(h, y):
-        return remote(
-            streams.at[:, pl.ds(rows - flen, flen), half_lanes(y, h)],
-            buf.at[:, pl.ds(0, flen), lanes_of(h)],
-            halo_send.at[y, h],
-            halo_recv.at[h],
-            place(lax.rem(layer + 1, LAYERS), y),
-        )
-
-    def kv_copy(h):
-        return remote(
-            feat.at[pl.ds(1, 2), :, lanes_of(h)],
-            far_kv.at[:, :, lanes_of(h)],
-            kv_send.at[h],
-            kv_recv.at[h],
+    def halo_copy(s, h):
+        return remote(
+            buf.at[s, pl.ds(span, flen), lanes_of(h)],
+            buf.at[s, pl.ds(0, flen), lanes_of(h)],
+            halo_send.at[s, h],
+            halo_recv.at[s, h],
+            place(lax.rem(layer + 1, LAYERS), side),
+        )
+
+    def own_halo_copy(s, h):
+        return remote(
+            streams.at[s, pl.ds(rows - flen, flen), half_lanes(side, h)],
+            buf.at[s, pl.ds(0, flen), lanes_of(h)],
+            halo_send.at[s, h],
+            halo_recv.at[s, h],
+            place(lax.rem(layer + 1, LAYERS), side),
+        )
+
+    def kv_copy(j, h):
+        return remote(
+            feat.at[1 + j, :, lanes_of(h)],
+            far_kv.at[j, :, lanes_of(h)],
+            kv_send.at[j, h],
+            kv_recv.at[j, h],
             place(HUB, side),
         )
 
@@ -178,20 +190,71 @@
     own_copy().start()
     pl.semaphore_wait(barrier, n - 1 + n_grp - 1)
 
-    lead = jnp.where(layer <= HUB, 1, 0)
-
-    def stream_at(j):
-        return lax.rem(j + lead, 3)
-
-    @pl.loop(0, heads)
-    def _(h):
-        for j in range(3):
-            side_copy(stream_at(j), h, side).start()
-
-        @pl.when((side == SIDES - 1) & (layer < LAYERS - 1))
-        def _():
-            for y in range(SIDES):
-                halo_copy(h, y).start()
+    last = layer == LAYERS - 1
+    sends_own_halo = (side == SIDES - 1) & jnp.logical_not(last)
+    passes_halo = (side < SIDES - 1) & jnp.logical_not(last)
+
+    def send_side(s, h):
+        for p in range(2):
+            side_copy(s, h, p).start()
+
+    @pl.when(layer == 0)
+    def _():
+        @pl.loop(0, heads)
+        def _(h):
+            send_side(1, h)
+            send_side(2, h)
+
+            @pl.when(h == 0)
+            def _():
+                for k in range(heads):
+                    side_copy(0, k, 0).start()
+
+        @pl.loop(0, heads)
+        def _(h):
+            side_copy(0, h, 1).start()
+
+    @pl.when(layer == HUB)
+    def _():
+        @pl.loop(0, heads)
+        def _(h):
+            side_copy(0, h, 0).start()
+
+        @pl.loop(0, heads)
+        def _(h):
+            send_side(1, h)
+            send_side(2, h)
+            side_copy(0, h, 1).start()
+
+    @pl.when(layer > HUB)
+    def _():
+        @pl.loop(0, heads)
+        def _(h):
+            send_side(0, h)
+
+        @pl.loop(0, heads)
+        def _(h):
+            send_side(1, h)
+            send_side(2, h)
+
+    @pl.when(sends_own_halo & (layer == 0))
+    def _():
+        @pl.loop(0, heads)
+        def _(h):
+            own_halo_copy(1, h).start()
+            own_halo_copy(2, h).start()
+            own_halo_copy(0, h).start()
+
+    @pl.when(sends_own_halo & (layer > 0))
+    def _():
+        @pl.loop(0, heads)
+        def _(h):
+            own_halo_copy(0, h).start()
+
+        @pl.loop(0, heads)
+        def _(h):
+            own_halo_copy(1, h).start()
+            own_halo_copy(2, h).start()
 
     @pl.when(layer == 0)
     def _():
@@ -211,23 +274,17 @@
             preferred_element_type=jnp.float32,
         )
 
-    def build(h):
-        @pl.loop(0, 3)
-        def _(s):
-            lines = turned[s, pl.ds(pl.multiple_of(h * per_tile, per_tile), per_tile), :]
-            for g in range(per_tile):
-                table = pltpu.roll(
-                    jnp.broadcast_to(lines[g : g + 1], (flen, flen)),
-                    0,
-                    1,
-                    stride=1,
-                    stride_axis=0,
-                )
-                lower = jnp.where(col_id <= row_id, table, 0.0)
-                upper = jnp.where(col_id > row_id, table, 0.0)
-                where = pl.ds(g * flen, flen)
-                toep[s, where, pl.ds(0, flen)] = upper.astype(toep.dtype)
-                toep[s, where, pl.ds(flen, flen)] = lower.astype(toep.dtype)
+    def build(s, h):
+        lines = turned[s, pl.ds(pl.multiple_of(h * per_tile, per_tile), per_tile), :]
+        for g in range(per_tile):
+            table = pltpu.roll(
+                jnp.broadcast_to(lines[g : g + 1], (flen, flen)), 0, 1, stride=1, stride_axis=0
+            )
+            lower = jnp.where(col_id <= row_id, table, 0.0)
+            upper = jnp.where(col_id > row_id, table, 0.0)
+            where = pl.ds(g * flen, flen)
+            toep[where, pl.ds(0, flen)] = upper.astype(toep.dtype)
+            toep[where, pl.ds(flen, flen)] = lower.astype(toep.dtype)
 
     blocks = span // flen
     lane_group = lax.broadcasted_iota(jnp.int32, (flen, blocks * LANES), 1)
@@ -243,7 +300,7 @@
         lanes = lanes_of(h)
         window = [buf[s, pl.ds(b * flen, 2 * flen), lanes] for b in range(blocks)]
         product = jnp.dot(
-            toep[s], jnp.concatenate(window, axis=1), preferred_element_type=jnp.float32
+            toep[...], jnp.concatenate(window, axis=1), preferred_element_type=jnp.float32
         )
         result = product[:flen]
         for g in range(1, per_tile):
@@ -251,6 +308,25 @@
         result = result.astype(feat.dtype)
         for b in range(blocks):
             feat[s, pl.ds(b * flen, flen), lanes] = result[:, b * LANES : (b + 1) * LANES]
+
+    def take_tail(s, h):
+        side_copy(s, h, 0).wait_recv()
+
+        @pl.when(passes_halo)
+        def _():
+            halo_copy(s, h).start()
+
+    def step(s, h, tail=True):
+        build(s, h)
+        if tail:
+            take_tail(s, h)
+        side_copy(s, h, 1).wait_recv()
+
+        @pl.when(layer > 0)
+        def _():
+            halo_copy(s, h).wait_recv()
+
+        filter_head(s, h)
 
     def attend(query, pieces):
         parts = []
@@ -338,63 +414,87 @@
             finish(h, r, (mixed / total).astype(jnp.bfloat16))
         back_copy(h, side).start()
 
-    @pl.loop(0, heads)
-    def _(h):
-        build(h)
-
-        @pl.when(h == 0)
-        def _():
-            own_copy().wait()
-
-        @pl.when(layer > 0)
-        def _():
-            halo_copy(h, 0).wait_recv()
-
-        @pl.loop(0, 3)
-        def _(j):
-            s = stream_at(j)
-            side_copy(s, h, side).wait_recv()
-            filter_head(s, h)
-
-            @pl.when((layer == 0) & (j == 1))
+    own_copy().wait()
+
+    @pl.when(layer == 0)
+    def _():
+        @pl.loop(0, heads)
+        def _(h):
+            @pl.loop(0, 2)
+            def _(j):
+                step(1 + j, h)
+                kv_copy(j, h).start()
+
+            @pl.when(h == 0)
             def _():
-                kv_copy(h).start()
-
-            @pl.when((layer == LAYERS - 1) & (j == 0))
-            def _():
-                q_copy(1, h).start()
-
-            @pl.when((layer > HUB) & (j == 0))
-            def _():
-                q_copy(0, h).start()
-
-        @pl.when(layer == 0)
-        def _():
+                for k in range(heads):
+                    take_tail(0, k)
+
+        @pl.loop(0, heads)
+        def _(h):
+            step(0, h, False)
             for r in range(SIDES):
                 mixed, _, total = attend(query_of(h, r), own_pieces(h, r))
                 finish(h, r, (mixed / total).astype(jnp.bfloat16))
             back_copy(h, side).start()
 
-        @pl.when(layer == HUB)
-        def _():
-            kv_copy(h).wait_recv()
+    @pl.when(layer == HUB)
+    def _():
+        @pl.loop(0, heads)
+        def _(h):
+            take_tail(0, h)
+
+        for j in range(2):
+            take_tail(1 + j, 0)
+
+        @pl.loop(0, heads)
+        def _(h):
+            @pl.loop(0, 2)
+            def _(j):
+                step(1 + j, h, False)
+
+            @pl.when(h + 1 < heads)
+            def _():
+                for j in range(2):
+                    take_tail(1 + j, h + 1)
+
+            for j in range(2):
+                kv_copy(j, h).wait_recv()
+
+            @pl.loop(0, LAYERS - 1 - HUB)
+            def _(d):
+                serve(d, h, [piece(far_kv, 0, h, 0, span), piece(feat, 1, h, 0, span)])
+
+            step(0, h, False)
             far = piece(far_kv, 0, h, 0, span)
             for r in range(SIDES):
                 mixed, _, total = attend(query_of(h, r), [far] + own_pieces(h, r))
                 finish(h, r, (mixed / total).astype(jnp.bfloat16))
             back_copy(h, side).start()
 
-            @pl.loop(0, LAYERS - 1 - HUB)
-            def _(d):
-                serve(d, h, [piece(far_kv, 0, h, 0, span), piece(feat, 1, h, 0, span)])
-
-        @pl.when(layer > HUB)
-        def _():
+    @pl.when(layer > HUB)
+    def _():
+        @pl.loop(0, heads)
+        def _(h):
+            step(0, h)
+
+            @pl.when(last)
+            def _():
+                q_copy(1, h).start()
+
+            q_copy(0, h).start()
+
+        @pl.loop(0, heads)
+        def _(h):
+            @pl.loop(0, 2)
+            def _(j):
+                step(1 + j, h)
+
             keep(h)
 
-        @pl.when((layer > HUB) & (layer < LAYERS - 1))
-        def _():
-            serve(0, h, [piece(feat, 1, h, 0, span)])
+            @pl.when(jnp.logical_not(last))
+            def _():
+                serve(0, h, [piece(feat, 1, h, 0, span)])
 
     @pl.when(layer == LAYERS - 2)
     def _():
@@ -452,17 +552,19 @@
     @pl.loop(0, heads)
     def _(h):
         for s in range(3):
-            side_copy(s, h, side).wait_send()
+            for p in range(2):
+                side_copy(s, h, p).wait_send()
         back_copy(h, side).wait_send()
 
-        @pl.when((side == SIDES - 1) & (layer < LAYERS - 1))
-        def _():
-            for y in range(SIDES):
-                halo_copy(h, y).wait_send()
+        @pl.when(jnp.logical_not(last))
+        def _():
+            for s in range(3):
+                halo_copy(s, h).wait_send()
 
         @pl.when(layer == 0)
         def _():
-            kv_copy(h).wait_send()
+            for j in range(2):
+                kv_copy(j, h).wait_send()
 
         @pl.when(layer > HUB)
         def _():
@@ -505,7 +607,7 @@
         scratch_shapes=[
             pltpu.VMEM((3, flen + span, half), low),
             pltpu.VMEM((3, groups // SIDES, flen), jnp.float32),
-            pltpu.VMEM((3, per_tile * flen, 2 * flen), low),
+            pltpu.VMEM((per_tile * flen, 2 * flen), low),
             pltpu.VMEM((3, span, half), low),
             pltpu.VMEM((2, span, half), low),
             pltpu.VMEM((far, span, half), low),
@@ -520,12 +622,12 @@
             pltpu.VMEM((rows, chans), low),
             pltpu.VMEM((n_grp, 8, rows), jnp.float32),
             dma((1,)),
+            dma((3, heads, 2)),
+            dma((3, heads, 2)),
             dma((3, heads)),
             dma((3, heads)),
-            dma((SIDES, heads)),
-            dma((heads,)),
-            dma((heads,)),
-            dma((heads,)),
+            dma((2, heads)),
+            dma((2, heads)),
             dma((far, heads)),
             dma((far, heads)),
             dma((far, heads, SIDES)),

time: 87.1 us -> 76.7 us (0.88)
  Pallas kernels: 84.8 us -> 74.4 us
    pallas_call x1, Pallas kernels: 84.8 us -> 74.4 us  [layered(): pl.pallas_call(functools.partial(layered_kernel, n, n_grp), out_shape=jax...]
where the time goes in v2:
time: 76.7 us; the launch traced here: 76.5 us
  Pallas kernels  74.4 us (97%)
  local copies, waits for them, and re-layouts  2.06 us (3%)
    pallas_call x1, Pallas kernels, layered(): pl.pallas_call(functools.partial(layered_kernel, n, n_grp), out_shape=jax...  74.4 us
    unnamed x1, local copies, waits for them, and re-layouts  2.06 us

profile of v2, /device:TPU:25, one launch (start us, length us, event | category | flops | bytes accessed | tf_op | source)
XLA Modules:
  0.0 76.5 jit_solution(7787526450618090829)
XLA Ops:
  0.0 74.4 %layered.1 = bf16[384,1024]{1,0:T(8,128)(2,1)} custom-call(bf16[3,384,1024]{2,1,0:T(8,128)(2,1)} %streams.1, bf16[3,64,128]{2,1,0:T(8,128)(2,1)} %filters.1, f32[1,1024]{1,0:T(1,128)} %bitcast.1), custom_call_target="tpu_custom_call" | custom-call | tf_op jit(solution)/shard_map/layered/pallas_call | solution.py:602
  74.4 2.1 %copy.5 = bf16[384,1024]{1,0:T(8,128)(2,1)} copy(bf16[384,1024]{1,0:T(8,128)(2,1)} %layered.1) | data formatting | bytes 1572864

commit v3 on v2

--- a/solution.py
+++ b/solution.py
@@ -132,12 +132,15 @@
             place(lax.rem(layer + 1, LAYERS), side),
         )
 
-    def kv_copy(j, h):
-        return remote(
-            feat.at[1 + j, :, lanes_of(h)],
-            far_kv.at[j, :, lanes_of(h)],
-            kv_send.at[j, h],
-            kv_recv.at[j, h],
+    def rows_of(r):
+        return pl.ds(pl.multiple_of(r * rows, flen), rows)
+
+    def kv_copy(j, h, r):
+        return remote(
+            feat.at[1 + j, rows_of(r), lanes_of(h)],
+            far_kv.at[j, rows_of(r), lanes_of(h)],
+            kv_send.at[j, h, r],
+            kv_recv.at[j, h, r],
             place(HUB, side),
         )
 
@@ -151,10 +154,9 @@
         )
 
     def part_copy(d, h, r):
-        where = pl.ds(r * rows, rows)
-        return remote(
-            part.at[d, where, lanes_of(h)],
-            inbox.at[d, where, lanes_of(h)],
+        return remote(
+            part.at[d, rows_of(r), lanes_of(h)],
+            inbox.at[d, rows_of(r), lanes_of(h)],
             part_send.at[d, h, r],
             part_recv.at[d, h, r],
             place(lax.rem(layer + d + 1, LAYERS), side),
@@ -162,8 +164,8 @@
 
     def stat_copy(d, h, r):
         return remote(
-            part_stat.at[d, h, r],
-            in_stat.at[d, h, r],
+            part_stat.at[d, h, r, pl.ds(0, 2)],
+            in_stat.at[d, h, r, pl.ds(0, 2)],
             stat_send.at[d, h, r],
             stat_recv.at[d, h, r],
             place(lax.rem(layer + d + 1, LAYERS), side),
@@ -204,11 +206,7 @@
         def _(h):
             send_side(1, h)
             send_side(2, h)
-
-            @pl.when(h == 0)
-            def _():
-                for k in range(heads):
-                    side_copy(0, k, 0).start()
+            side_copy(0, h, 0).start()
 
         @pl.loop(0, heads)
         def _(h):
@@ -219,31 +217,32 @@
         @pl.loop(0, heads)
         def _(h):
             side_copy(0, h, 0).start()
+
+        @pl.loop(0, heads)
+        def _(h):
+            for s in (1, 2):
+                side_copy(s, h, 0).start()
+
+        @pl.loop(0, heads)
+        def _(h):
+            for s in (1, 2, 0):
+                side_copy(s, h, 1).start()
+
+    @pl.when(layer > HUB)
+    def _():
+        @pl.loop(0, heads)
+        def _(h):
+            send_side(0, h)
 
         @pl.loop(0, heads)
         def _(h):
             send_side(1, h)
             send_side(2, h)
-            side_copy(0, h, 1).start()
-
-    @pl.when(layer > HUB)
-    def _():
-        @pl.loop(0, heads)
-        def _(h):
-            send_side(0, h)
-
-        @pl.loop(0, heads)
-        def _(h):
-            send_side(1, h)
-            send_side(2, h)
 
     @pl.when(sends_own_halo & (layer == 0))
     def _():
-        @pl.loop(0, heads)
-        def _(h):
-            own_halo_copy(1, h).start()
-            own_halo_copy(2, h).start()
-            own_halo_copy(0, h).start()
+        for s in range(3):
+            own_halo_copy(s, 0).start()
 
     @pl.when(sends_own_halo & (layer > 0))
     def _():
@@ -296,18 +295,20 @@
             result = op(result, values[:, c * LANES : (c + 1) * LANES])
         return result
 
-    def filter_head(s, h):
+    def filter_rows(s, h, first, count):
         lanes = lanes_of(h)
-        window = [buf[s, pl.ds(b * flen, 2 * flen), lanes] for b in range(blocks)]
+        starts = [pl.multiple_of(first + b * flen, flen) for b in range(count)]
+        window = [buf[s, pl.ds(start, 2 * flen), lanes] for start in starts]
         product = jnp.dot(
             toep[...], jnp.concatenate(window, axis=1), preferred_element_type=jnp.float32
         )
         result = product[:flen]
+        group = lane_group[:, : count * LANES]
         for g in range(1, per_tile):
-            result = jnp.where(lane_group == g, product[g * flen : (g + 1) * flen], result)
+            result = jnp.where(group == g, product[g * flen : (g + 1) * flen], result)
         result = result.astype(feat.dtype)
-        for b in range(blocks):
-            feat[s, pl.ds(b * flen, flen), lanes] = result[:, b * LANES : (b + 1) * LANES]
+        for b, start in enumerate(starts):
+            feat[s, pl.ds(start, flen), lanes] = result[:, b * LANES : (b + 1) * LANES]
 
     def take_tail(s, h):
         side_copy(s, h, 0).wait_recv()
@@ -326,7 +327,7 @@
         def _():
             halo_copy(s, h).wait_recv()
 
-        filter_head(s, h)
+        filter_rows(s, h, 0, blocks)
 
     def attend(query, pieces):
         parts = []
@@ -361,29 +362,30 @@
     def query_of(h, r):
         return feat[0, pl.ds(r * rows, rows), lanes_of(h)]
 
-    def finish(h, r, values):
-        @pl.when(side == r)
-        def _():
-            att[:, half_lanes(side, h)] = values
-
-        @pl.when(side != r)
-        def _():
-            sending[:, lanes_of(h)] = values
+    def finish(h, values):
+        for r in range(SIDES):
+            @pl.when(side == r)
+            def _():
+                att[:, half_lanes(side, h)] = values[r]
+                sending[:, lanes_of(h)] = values[1 - r]
 
     lane_id = lax.broadcasted_iota(jnp.int32, (rows, LANES), 1)
 
-    def serve(d, h, pieces):
-        q_copy(d, h).wait_recv()
-        results = [
-            attend(far_q[d, pl.ds(r * rows, rows), lanes_of(h)], pieces) for r in range(SIDES)
-        ]
-        for r, (mixed, top, total) in enumerate(results):
-            part[d, pl.ds(r * rows, rows), lanes_of(h)] = (mixed / total).astype(part.dtype)
-            stat = jnp.where(lane_id == 0, top, total)
-            part_stat[d, h, r] = stat.T[:8]
-        for r in range(SIDES):
-            part_copy(d, h, r).start()
-            stat_copy(d, h, r).start()
+    def serve(count, h, pieces):
+        for d in range(count):
+            q_copy(d, h).wait_recv()
+
+        @pl.loop(0, SIDES)
+        def _(i):
+            r = lax.rem(other + i, SIDES)
+            results = [
+                attend(far_q[d, rows_of(r), lanes_of(h)], pieces) for d in range(count)
+            ]
+            for d, (mixed, top, total) in reversed(list(enumerate(results))):
+                part[d, rows_of(r), lanes_of(h)] = (mixed / total).astype(part.dtype)
+                part_stat[d, h, r] = jnp.where(lane_id == 0, top, total).T[:8]
+                part_copy(d, h, r).start()
+                stat_copy(d, h, r).start()
 
     def keep(h):
         for r in range(SIDES):
@@ -396,12 +398,12 @@
         return jnp.broadcast_to(line, (LANES, rows)).T
 
     def merge(h, count):
-        for r in range(SIDES):
+        @pl.loop(0, SIDES)
+        def _(i):
+            r = lax.rem(other + i, SIDES)
             for d in range(count):
                 part_copy(d, h, r).wait_recv()
                 stat_copy(d, h, r).wait_recv()
-        for r in range(SIDES):
-            where = pl.ds(r * rows, rows)
             tops = [own_top[h, r]] + [spread(in_stat[d, h, r, 0:1, :]) for d in range(count)]
             totals = [own_total[h, r]] + [spread(in_stat[d, h, r, 1:2, :]) for d in range(count)]
             top = functools.reduce(jnp.maximum, tops)
@@ -409,92 +411,112 @@
             total = functools.reduce(jnp.add, [a * b for a, b in zip(scales, totals)])
             mixed = own_acc[h, r] * scales[0]
             for d in range(count):
-                values = inbox[d, where, lanes_of(h)].astype(jnp.float32)
+                values = inbox[d, rows_of(r), lanes_of(h)].astype(jnp.float32)
                 mixed = mixed + values * (scales[d + 1] * totals[d + 1])
-            finish(h, r, (mixed / total).astype(jnp.bfloat16))
-        back_copy(h, side).start()
+            values = (mixed / total).astype(jnp.bfloat16)
+
+            @pl.when(i == 0)
+            def _():
+                sending[:, lanes_of(h)] = values
+                back_copy(h, side).start()
+
+            @pl.when(i > 0)
+            def _():
+                att[:, half_lanes(side, h)] = values
 
     own_copy().wait()
 
     @pl.when(layer == 0)
     def _():
+        @pl.loop(0, heads)
+        def _(h):
+            @pl.loop(0, 2)
+            def _(j):
+                build(1 + j, h)
+
+                @pl.loop(0, SIDES)
+                def _(i):
+                    r = lax.rem(side + i, SIDES)
+
+                    @pl.when(i != side)
+                    def _():
+                        take_tail(1 + j, h)
+
+                    @pl.when(i > 0)
+                    def _():
+                        side_copy(1 + j, h, 1).wait_recv()
+
+                    filter_rows(1 + j, h, r * rows, rows // flen)
+                    kv_copy(j, h, r).start()
+
+            take_tail(0, h)
+
+            @pl.when((side == SIDES - 1) & (h + 1 < heads))
+            def _():
+                for s in range(3):
+                    own_halo_copy(s, h + 1).start()
+
+        @pl.loop(0, heads)
+        def _(h):
+            step(0, h, False)
+            results = [attend(query_of(h, r), own_pieces(h, r)) for r in range(SIDES)]
+            finish(h, [(mixed / total).astype(jnp.bfloat16) for mixed, _, total in results])
+            back_copy(h, side).start()
+
+    @pl.when(layer == HUB)
+    def _():
+        @pl.loop(0, heads)
+        def _(h):
+            take_tail(0, h)
+
+        @pl.loop(0, heads)
+        def _(h):
+            for j in range(2):
+                take_tail(1 + j, h)
+
+        @pl.loop(0, heads)
+        def _(h):
+            @pl.loop(0, 2)
+            def _(j):
+                step(1 + j, h, False)
+
+            for j in range(2):
+                for r in range(SIDES):
+                    kv_copy(j, h, r).wait_recv()
+
+            serve(
+                LAYERS - 1 - HUB, h, [piece(far_kv, 0, h, 0, span), piece(feat, 1, h, 0, span)]
+            )
+
+            step(0, h, False)
+            far = piece(far_kv, 0, h, 0, span)
+            results = [attend(query_of(h, r), [far] + own_pieces(h, r)) for r in range(SIDES)]
+            finish(h, [(mixed / total).astype(jnp.bfloat16) for mixed, _, total in results])
+            back_copy(h, side).start()
+
+    @pl.when(layer > HUB)
+    def _():
+        @pl.loop(0, heads)
+        def _(h):
+            step(0, h)
+
+            @pl.when(last)
+            def _():
+                q_copy(1, h).start()
+
+            q_copy(0, h).start()
+
         @pl.loop(0, heads)
         def _(h):
             @pl.loop(0, 2)
             def _(j):
                 step(1 + j, h)
-                kv_copy(j, h).start()
-
-            @pl.when(h == 0)
-            def _():
-                for k in range(heads):
-                    take_tail(0, k)
-
-        @pl.loop(0, heads)
-        def _(h):
-            step(0, h, False)
-            for r in range(SIDES):
-                mixed, _, total = attend(query_of(h, r), own_pieces(h, r))
-                finish(h, r, (mixed / total).astype(jnp.bfloat16))
-            back_copy(h, side).start()
-
-    @pl.when(layer == HUB)
-    def _():
-        @pl.loop(0, heads)
-        def _(h):
-            take_tail(0, h)
-
-        for j in range(2):
-            take_tail(1 + j, 0)
-
-        @pl.loop(0, heads)
-        def _(h):
-            @pl.loop(0, 2)
-            def _(j):
-                step(1 + j, h, False)
-
-            @pl.when(h + 1 < heads)
-            def _():
-                for j in range(2):
-                    take_tail(1 + j, h + 1)
-
-            for j in range(2):
-                kv_copy(j, h).wait_recv()
-
-            @pl.loop(0, LAYERS - 1 - HUB)
-            def _(d):
-                serve(d, h, [piece(far_kv, 0, h, 0, span), piece(feat, 1, h, 0, span)])
-
-            step(0, h, False)
-            far = piece(far_kv, 0, h, 0, span)
-            for r in range(SIDES):
-                mixed, _, total = attend(query_of(h, r), [far] + own_pieces(h, r))
-                finish(h, r, (mixed / total).astype(jnp.bfloat16))
-            back_copy(h, side).start()
-
-    @pl.when(layer > HUB)
-    def _():
-        @pl.loop(0, heads)
-        def _(h):
-            step(0, h)
-
-            @pl.when(last)
-            def _():
-                q_copy(1, h).start()
-
-            q_copy(0, h).start()
-
-        @pl.loop(0, heads)
-        def _(h):
-            @pl.loop(0, 2)
-            def _(j):
-                step(1 + j, h)
 
             keep(h)
 
             @pl.when(jnp.logical_not(last))
             def _():
-                serve(0, h, [piece(feat, 1, h, 0, span)])
+                serve(1, h, [piece(feat, 1, h, 0, span)])
 
     @pl.when(layer == LAYERS - 2)
     def _():
@@ -564,7 +586,8 @@
         @pl.when(layer == 0)
         def _():
             for j in range(2):
-                kv_copy(j, h).wait_send()
+                for r in range(SIDES):
+                    kv_copy(j, h, r).wait_send()
 
         @pl.when(layer > HUB)
         def _():
@@ -626,8 +649,8 @@
             dma((3, heads, 2)),
             dma((3, heads)),
             dma((3, heads)),
-            dma((2, heads)),
-            dma((2, heads)),
+            dma((2, heads, SIDES)),
+            dma((2, heads, SIDES)),
             dma((far, heads)),
             dma((far, heads)),
             dma((far, heads, SIDES)),

time: 76.7 us -> 73.1 us (0.953)
  the two profiles are of different devices: /device:TPU:25 before, /device:TPU:29 now
where the time goes in v3:
time: 73.1 us; the launch traced here: 72.9 us
  Pallas kernels  70.8 us (97%)
  local copies, waits for them, and re-layouts  2.06 us (3%)
    pallas_call x1, Pallas kernels, layered(): pl.pallas_call(functools.partial(layered_kernel, n, n_grp), out_shape=jax...  70.8 us
    unnamed x1, local copies, waits for them, and re-layouts  2.06 us

profile of v3, /device:TPU:29, one launch (start us, length us, event | category | flops | bytes accessed | tf_op | source)
XLA Modules:
  0.0 72.9 jit_solution(16976862103316935928)
XLA Ops:
  0.0 70.8 %layered.1 = bf16[384,1024]{1,0:T(8,128)(2,1)} custom-call(bf16[3,384,1024]{2,1,0:T(8,128)(2,1)} %streams.1, bf16[3,64,128]{2,1,0:T(8,128)(2,1)} %filters.1, f32[1,1024]{1,0:T(1,128)} %bitcast.1), custom_call_target="tpu_custom_call" | custom-call | tf_op jit(solution)/shard_map/layered/pallas_call | solution.py:625
  70.8 2.1 %copy.5 = bf16[384,1024]{1,0:T(8,128)(2,1)} copy(bf16[384,1024]{1,0:T(8,128)(2,1)} %layered.1) | data formatting | bytes 1572864

commit v4 on v3

--- a/solution.py
+++ b/solution.py
@@ -181,16 +181,23 @@
         )
 
     barrier = pltpu.get_barrier_semaphore()
-    for k in range(1, n):
-        pl.semaphore_signal(
-            barrier, inc=1, device_id={"ctx": lax.rem(me + k, n)}, device_id_type=MESH
-        )
+
+    def greet(device):
+        pl.semaphore_signal(barrier, inc=1, device_id=device, device_id_type=MESH)
+
+    greet(place(layer, other))
+    for k in range(1, LAYERS):
+        partner = lax.rem(layer + k, LAYERS)
+
+        @pl.when((partner == HUB) | (layer == HUB) | ((partner > 0) & (layer > 0)))
+        def _():
+            greet(place(partner, side))
+
     for k in range(1, n_grp):
-        pl.semaphore_signal(
-            barrier, inc=1, device_id={"grp": lax.rem(my_grp + k, n_grp)}, device_id_type=MESH
-        )
+        greet({"grp": lax.rem(my_grp + k, n_grp)})
+    partners = jnp.where(layer == 0, 1, jnp.where(layer == HUB, LAYERS - 1, LAYERS - 2))
     own_copy().start()
-    pl.semaphore_wait(barrier, n - 1 + n_grp - 1)
+    pl.semaphore_wait(barrier, partners + n_grp)
 
     last = layer == LAYERS - 1
     sends_own_halo = (side == SIDES - 1) & jnp.logical_not(last)
@@ -236,8 +243,13 @@
 
         @pl.loop(0, heads)
         def _(h):
-            send_side(1, h)
-            send_side(2, h)
+            for s in (1, 2):
+                side_copy(s, h, 0).start()
+
+        @pl.loop(0, heads)
+        def _(h):
+            for s in (1, 2):
+                side_copy(s, h, 1).start()
 
     @pl.when(sends_own_halo & (layer == 0))
     def _():
@@ -508,9 +520,14 @@
 
         @pl.loop(0, heads)
         def _(h):
+            for j in range(2):
+                take_tail(1 + j, h)
+
+        @pl.loop(0, heads)
+        def _(h):
             @pl.loop(0, 2)
             def _(j):
-                step(1 + j, h)
+                step(1 + j, h, False)
 
             keep(h)
 

time: 73.1 us -> 68.9 us (0.943)
  the two profiles are of different devices: /device:TPU:29 before, /device:TPU:25 now
where the time goes in v4:
time: 68.9 us; the launch traced here: 68.1 us
  Pallas kernels  66 us (96%)
  local copies, waits for them, and re-layouts  2.06 us (3%)
    pallas_call x1, Pallas kernels, layered(): pl.pallas_call(functools.partial(layered_kernel, n, n_grp), out_shape=jax...  66 us
    unnamed x1, local copies, waits for them, and re-layouts  2.06 us

profile of v4, /device:TPU:25, one launch (start us, length us, event | category | flops | bytes accessed | tf_op | source)
XLA Modules:
  0.0 68.1 jit_solution(12461264479409274159)
XLA Ops:
  0.0 66.0 %layered.1 = bf16[384,1024]{1,0:T(8,128)(2,1)} custom-call(bf16[3,384,1024]{2,1,0:T(8,128)(2,1)} %streams.1, bf16[3,64,128]{2,1,0:T(8,128)(2,1)} %filters.1, f32[1,1024]{1,0:T(1,128)} %bitcast.1), custom_call_target="tpu_custom_call" | custom-call | tf_op jit(solution)/shard_map/layered/pallas_call | solution.py:642
  66.0 2.1 %copy.5 = bf16[384,1024]{1,0:T(8,128)(2,1)} copy(bf16[384,1024]{1,0:T(8,128)(2,1)} %layered.1) | data formatting | bytes 1572864

commit v5 on v4

--- a/solution.py
+++ b/solution.py
@@ -15,6 +15,7 @@
 SIDES = 2
 LAYERS = 4
 HUB = 1
+FAR = LAYERS - 1 - HUB
 
 
 def layered_kernel(
@@ -197,75 +198,6 @@
         greet({"grp": lax.rem(my_grp + k, n_grp)})
     partners = jnp.where(layer == 0, 1, jnp.where(layer == HUB, LAYERS - 1, LAYERS - 2))
     own_copy().start()
-    pl.semaphore_wait(barrier, partners + n_grp)
-
-    last = layer == LAYERS - 1
-    sends_own_halo = (side == SIDES - 1) & jnp.logical_not(last)
-    passes_halo = (side < SIDES - 1) & jnp.logical_not(last)
-
-    def send_side(s, h):
-        for p in range(2):
-            side_copy(s, h, p).start()
-
-    @pl.when(layer == 0)
-    def _():
-        @pl.loop(0, heads)
-        def _(h):
-            send_side(1, h)
-            send_side(2, h)
-            side_copy(0, h, 0).start()
-
-        @pl.loop(0, heads)
-        def _(h):
-            side_copy(0, h, 1).start()
-
-    @pl.when(layer == HUB)
-    def _():
-        @pl.loop(0, heads)
-        def _(h):
-            side_copy(0, h, 0).start()
-
-        @pl.loop(0, heads)
-        def _(h):
-            for s in (1, 2):
-                side_copy(s, h, 0).start()
-
-        @pl.loop(0, heads)
-        def _(h):
-            for s in (1, 2, 0):
-                side_copy(s, h, 1).start()
-
-    @pl.when(layer > HUB)
-    def _():
-        @pl.loop(0, heads)
-        def _(h):
-            send_side(0, h)
-
-        @pl.loop(0, heads)
-        def _(h):
-            for s in (1, 2):
-                side_copy(s, h, 0).start()
-
-        @pl.loop(0, heads)
-        def _(h):
-            for s in (1, 2):
-                side_copy(s, h, 1).start()
-
-    @pl.when(sends_own_halo & (layer == 0))
-    def _():
-        for s in range(3):
-            own_halo_copy(s, 0).start()
-
-    @pl.when(sends_own_halo & (layer > 0))
-    def _():
-        @pl.loop(0, heads)
-        def _(h):
-            own_halo_copy(0, h).start()
-
-        @pl.loop(0, heads)
-        def _(h):
-            own_halo_copy(1, h).start()
-            own_halo_copy(2, h).start()
 
     @pl.when(layer == 0)
     def _():
@@ -285,6 +217,76 @@
             preferred_element_type=jnp.float32,
         )
 
+    pl.semaphore_wait(barrier, partners + n_grp)
+
+    last = layer == LAYERS - 1
+    sends_own_halo = (side == SIDES - 1) & jnp.logical_not(last)
+    passes_halo = (side < SIDES - 1) & jnp.logical_not(last)
+
+    def send_side(s, h):
+        for p in range(2):
+            side_copy(s, h, p).start()
+
+    @pl.when(layer == 0)
+    def _():
+        @pl.loop(0, heads)
+        def _(h):
+            send_side(1, h)
+            send_side(2, h)
+            side_copy(0, h, 0).start()
+
+        @pl.loop(0, heads)
+        def _(h):
+            side_copy(0, h, 1).start()
+
+    @pl.when(layer == HUB)
+    def _():
+        @pl.loop(0, heads)
+        def _(h):
+            side_copy(0, h, 0).start()
+
+        @pl.loop(0, heads)
+        def _(h):
+            for s in (1, 2):
+                side_copy(s, h, 0).start()
+
+        @pl.loop(0, heads)
+        def _(h):
+            for s in (1, 2, 0):
+                side_copy(s, h, 1).start()
+
+    @pl.when(layer > HUB)
+    def _():
+        @pl.loop(0, heads)
+        def _(h):
+            send_side(0, h)
+
+        @pl.loop(0, heads)
+        def _(h):
+            for s in (1, 2):
+                side_copy(s, h, 0).start()
+
+        @pl.loop(0, heads)
+        def _(h):
+            for s in (1, 2):
+                side_copy(s, h, 1).start()
+
+    @pl.when(sends_own_halo & (layer == 0))
+    def _():
+        for s in (1, 2):
+            own_halo_copy(s, 0).start()
+
+    @pl.when(sends_own_halo & (layer > 0))
+    def _():
+        @pl.loop(0, heads)
+        def _(h):
+            own_halo_copy(0, h).start()
+
+        @pl.loop(0, heads)
+        def _(h):
+            own_halo_copy(1, h).start()
+            own_halo_copy(2, h).start()
+
     def build(s, h):
         lines = turned[s, pl.ds(pl.multiple_of(h * per_tile, per_tile), per_tile), :]
         for g in range(per_tile):
@@ -328,6 +330,13 @@
         @pl.when(passes_halo)
         def _():
             halo_copy(s, h).start()
+
+    def pass_query_halo(h):
+        take_tail(0, h)
+
+        @pl.when(sends_own_halo)
+        def _():
+            own_halo_copy(0, h).start()
 
     def step(s, h, tail=True):
         build(s, h)
@@ -399,6 +408,33 @@
                 part_copy(d, h, r).start()
                 stat_copy(d, h, r).start()
 
+    def hub_serve(h):
+        for j in range(2):
+            for r in range(SIDES):
+                kv_copy(j, h, r).wait_recv()
+        for d in range(FAR):
+            q_copy(d, h).wait_recv()
+        pieces = [piece(far_kv, 0, h, 0, span), piece(feat, 1, h, 0, span)]
+
+        def answer(turns):
+            results = [
+                attend(far_q[d, rows_of(r), lanes_of(h)], pieces) for r, d in turns
+            ]
+            for (r, d), (mixed, top, total) in zip(turns, results):
+                part[d, rows_of(r), lanes_of(h)] = (mixed / total).astype(part.dtype)
+                part_stat[d, h, r] = jnp.where(lane_id == 0, top, total).T[:8]
+                part_copy(d, h, r).start()
+                stat_copy(d, h, r).start()
+
+        answer([(lax.rem(other + i, SIDES), FAR - 1 - d) for i in range(SIDES) for d in range(FAR)])
+
+    def hub_own(h):
+        step(0, h, False)
+        far = piece(far_kv, 0, h, 0, span)
+        results = [attend(query_of(h, r), [far] + own_pieces(h, r)) for r in range(SIDES)]
+        finish(h, [(mixed / total).astype(jnp.bfloat16) for mixed, _, total in results])
+        back_copy(h, side).start()
+
     def keep(h):
         for r in range(SIDES):
             mixed, top, total = attend(query_of(h, r), own_pieces(h, r))
@@ -461,12 +497,16 @@
                     filter_rows(1 + j, h, r * rows, rows // flen)
                     kv_copy(j, h, r).start()
 
-            take_tail(0, h)
-
-            @pl.when((side == SIDES - 1) & (h + 1 < heads))
+            @pl.when(sends_own_halo & (h + 1 < heads))
             def _():
-                for s in range(3):
+                for s in (1, 2):
                     own_halo_copy(s, h + 1).start()
+
+            @pl.when(h > 0)
+            def _():
+                pass_query_halo(h - 1)
+
+        pass_query_halo(heads - 1)
 
         @pl.loop(0, heads)
         def _(h):
@@ -492,32 +532,26 @@
             def _(j):
                 step(1 + j, h, False)
 
-            for j in range(2):
-                for r in range(SIDES):
-                    kv_copy(j, h, r).wait_recv()
-
-            serve(
-                LAYERS - 1 - HUB, h, [piece(far_kv, 0, h, 0, span), piece(feat, 1, h, 0, span)]
-            )
-
-            step(0, h, False)
-            far = piece(far_kv, 0, h, 0, span)
-            results = [attend(query_of(h, r), [far] + own_pieces(h, r)) for r in range(SIDES)]
-            finish(h, [(mixed / total).astype(jnp.bfloat16) for mixed, _, total in results])
-            back_copy(h, side).start()
+            hub_serve(h)
+
+            @pl.when(h > 0)
+            def _():
+                hub_own(h - 1)
+
+        hub_own(heads - 1)
 
     @pl.when(layer > HUB)
     def _():
         @pl.loop(0, heads)
         def _(h):
             step(0, h)
+
+            q_copy(0, h).start()
 
             @pl.when(last)
             def _():
                 q_copy(1, h).start()
 
-            q_copy(0, h).start()
-
         @pl.loop(0, heads)
         def _(h):
             for j in range(2):
@@ -529,11 +563,11 @@
             def _(j):
                 step(1 + j, h, False)
 
-            keep(h)
-
             @pl.when(jnp.logical_not(last))
             def _():
                 serve(1, h, [piece(feat, 1, h, 0, span)])
+
+            keep(h)
 
     @pl.when(layer == LAYERS - 2)
     def _():
@@ -638,7 +672,7 @@
     vmem = pl.BlockSpec(memory_space=pltpu.VMEM)
     dma = pltpu.SemaphoreType.DMA
     low = jnp.bfloat16
-    far = LAYERS - 1 - HUB
+    far = FAR
     return pl.pallas_call(
         functools.partial(layered_kernel, n, n_grp),
         out_shape=jax.ShapeDtypeStruct((rows, chans), low),

time: 68.9 us -> 68.2 us (0.990)
  the two profiles are of different devices: /device:TPU:25 before, /device:TPU:19 now
where the time goes in v5:
time: 68.2 us; the launch traced here: 68 us
  Pallas kernels  66 us (97%)
  local copies, waits for them, and re-layouts  2.06 us (3%)
    pallas_call x1, Pallas kernels, layered(): pl.pallas_call(functools.partial(layered_kernel, n, n_grp), out_shape=jax...  66 us
    unnamed x1, local copies, waits for them, and re-layouts  2.06 us

profile of v5, /device:TPU:19, one launch (start us, length us, event | category | flops | bytes accessed | tf_op | source)
XLA Modules:
  0.0 68.0 jit_solution(864484503381687288)
XLA Ops:
  0.0 66.0 %layered.1 = bf16[384,1024]{1,0:T(8,128)(2,1)} custom-call(bf16[3,384,1024]{2,1,0:T(8,128)(2,1)} %streams.1, bf16[3,64,128]{2,1,0:T(8,128)(2,1)} %filters.1, f32[1,1024]{1,0:T(1,128)} %bitcast.1), custom_call_target="tpu_custom_call" | custom-call | tf_op jit(solution)/shard_map/layered/pallas_call | solution.py:676
  66.0 2.1 %copy.5 = bf16[384,1024]{1,0:T(8,128)(2,1)} copy(bf16[384,1024]{1,0:T(8,128)(2,1)} %layered.1) | data formatting | bytes 1572864

commit v6 on v5

--- a/solution.py
+++ b/solution.py
@@ -426,7 +426,7 @@
                 part_copy(d, h, r).start()
                 stat_copy(d, h, r).start()
 
-        answer([(lax.rem(other + i, SIDES), FAR - 1 - d) for i in range(SIDES) for d in range(FAR)])
+        answer([(lax.rem(other + i, SIDES), (d + i) % FAR) for i in range(SIDES) for d in range(FAR)])
 
     def hub_own(h):
         step(0, h, False)

time: 68.2 us -> 68.3 us (level)
  the two profiles are of different devices: /device:TPU:19 before, /device:TPU:25 now
where the time goes in v6:
time: 68.3 us; the launch traced here: 67.1 us
  Pallas kernels  65 us (95%)
  local copies, waits for them, and re-layouts  2.06 us (3%)
    pallas_call x1, Pallas kernels, layered(): pl.pallas_call(functools.partial(layered_kernel, n, n_grp), out_shape=jax...  65 us
    unnamed x1, local copies, waits for them, and re-layouts  2.06 us

profile of v6, /device:TPU:25, one launch (start us, length us, event | category | flops | bytes accessed | tf_op | source)
XLA Modules:
  0.0 67.1 jit_solution(6952658583866334511)
XLA Ops:
  0.0 65.0 %layered.1 = bf16[384,1024]{1,0:T(8,128)(2,1)} custom-call(bf16[3,384,1024]{2,1,0:T(8,128)(2,1)} %streams.1, bf16[3,64,128]{2,1,0:T(8,128)(2,1)} %filters.1, f32[1,1024]{1,0:T(1,128)} %bitcast.1), custom_call_target="tpu_custom_call" | custom-call | tf_op jit(solution)/shard_map/layered/pallas_call | solution.py:676
  65.0 2.1 %copy.5 = bf16[384,1024]{1,0:T(8,128)(2,1)} copy(bf16[384,1024]{1,0:T(8,128)(2,1)} %layered.1) | data formatting | bytes 1572864
